TPU v7x, 512 devices: a whole 4x8x8 slice. The times are simulated.
512 devices in a mesh: dp: 16 (over y, core), expert: 8 (over z), tensor: 4 (over x).
Axes of the slice: x: 4, y: 8, z: 8, core: 2. Of those that a mesh axis runs over, the one named last changes fastest.
Arguments:
- tokens: bfloat16 [8192, 4096], P(('dp', 'expert'), 'tensor'), may hold values from -6 to 6
- expert_ids: int32 [8192, 8], P(('dp', 'expert')), may hold values from 0 to 127, all different within a row; in each aligned block of 64 rows (0 to 63, 64 to 127, ...) at most 6 rows name the same one
- combine_weights: float32 [8192, 8], P(('dp', 'expert')), may hold values from 0.05 to 1
- topology: int32 [128, 12, 12], P(('dp', 'expert'), 'tensor'), may hold values from 0 to 31, all different within a row
- gate_blocks: bfloat16 [128, 12, 12, 128, 128], P(('dp', 'expert'), 'tensor'), may hold values from -0.15625 to 0.15625
- up_blocks: bfloat16 [128, 12, 12, 128, 128], P(('dp', 'expert'), 'tensor'), may hold values from -0.15625 to 0.15625
- down_blocks: bfloat16 [128, 12, 12, 128, 128], P(('dp', 'expert'), 'tensor'), may hold values from -0.25 to 0.25
Outputs:
- layer_out: bfloat16 [8192, 4096], P(('dp', 'expert'), 'tensor')
Inputs may be any that keep to these rules, and one draw needn't show every extreme that they name: `expert_ids`: in each aligned block of 64 tokens (the tokens of one index of dp+expert), no expert is named more than 6 times, a bound that some block reaches; a token names 8 different experts. `topology`: each row names 12 different blocks; every block is named by some row.
All inputs are finite; a program needn't handle non-finite values.
Results may differ from a plain program's by a relative error of at most 0.0058.
Values may be sent and summed in bfloat16 or wider, within the bound.
A program may use at most 128 MiB of HBM per device.

v0:
```python
import jax
import jax.numpy as jnp
from jax import lax
from jax.sharding import PartitionSpec as P

D = 4096
TOP = 8
BLK = 128


def slot_numbers(expert_ids, experts):
    flat_ids = expert_ids.reshape(-1)
    onehot = (flat_ids[:, None] == jnp.arange(experts, dtype=jnp.int32)[None, :]).astype(jnp.int32)
    before = jnp.cumsum(onehot, axis=0) - onehot
    return jnp.sum(before * onehot, axis=1).reshape(expert_ids.shape)


def combine_rows(flat_rows, target, combine_weights):
    total = jnp.zeros((target.shape[0], flat_rows.shape[1]), jnp.float32)
    for pick in range(target.shape[1]):
        chosen = jnp.take(flat_rows, target[:, pick], axis=0)
        total = total + combine_weights[:, pick][:, None] * chosen
    return total


def per_device(tokens, expert_ids, combine_weights, topology, gate_blocks, up_blocks, down_blocks):
    experts = lax.axis_size(("dp", "expert"))
    tok_rows = tokens.shape[0]
    capacity = min(tok_rows, 3 * tok_rows * TOP // (2 * experts))
    slot_index = slot_numbers(expert_ids, experts)
    target = expert_ids * capacity + slot_index
    places = jnp.arange(experts * capacity, dtype=jnp.int32)
    matches = target[None, :, :] == places[:, None, None]
    dispatch = jnp.any(matches, axis=2).astype(jnp.bfloat16)
    outgoing = jnp.dot(dispatch, tokens, preferred_element_type=jnp.float32).astype(jnp.bfloat16)
    outgoing = outgoing.reshape(experts, capacity, tokens.shape[1])
    arrived = lax.all_to_all(outgoing, ("dp", "expert"), split_axis=0, concat_axis=0, tiled=True)
    expert_in = lax.all_gather(arrived, "tensor", axis=2, tiled=True)
    row_count = experts * capacity
    layout_ids = topology[0]
    local_blocks = layout_ids.shape[0]
    blocked = expert_in.reshape(row_count, D // BLK, BLK)
    width_ids = jnp.arange(D // BLK, dtype=jnp.int32)
    partial_value = jnp.zeros((row_count, D // BLK, BLK), jnp.float32)
    for block in range(local_blocks):
        chosen = layout_ids[block]
        picked = jnp.take(blocked, chosen, axis=1)
        gate_proj = jnp.einsum(
            "rkc,kcf->rf", picked, gate_blocks[0, block], preferred_element_type=jnp.float32
        )
        up_proj = jnp.einsum(
            "rkc,kcf->rf", picked, up_blocks[0, block], preferred_element_type=jnp.float32
        )
        hidden = (jax.nn.silu(gate_proj) * up_proj).astype(jnp.bfloat16)
        pieces = jnp.einsum(
            "rf,kfc->rkc", hidden, down_blocks[0, block], preferred_element_type=jnp.float32
        )
        placer = (chosen[:, None] == width_ids[None, :]).astype(jnp.float32)
        partial_value = partial_value + jnp.einsum(
            "rkc,kb->rbc", pieces, placer, precision=lax.Precision.HIGHEST
        )
    partial_low = lax.optimization_barrier(
        partial_value.reshape(experts, capacity, D).astype(jnp.bfloat16)
    )
    shares = lax.all_to_all(
        partial_low.reshape(1, experts, capacity, D),
        "tensor",
        split_axis=3,
        concat_axis=0,
        tiled=True,
    )
    summed = jnp.sum(shares.astype(jnp.float32), axis=0)
    returned_rows = lax.all_to_all(
        summed, ("dp", "expert"), split_axis=0, concat_axis=0, tiled=True
    )
    flat_rows = returned_rows.reshape(row_count, returned_rows.shape[2])
    combined = combine_rows(flat_rows, target, combine_weights)
    return combined.astype(jnp.bfloat16)


def solution(mesh):
    return jax.shard_map(
        per_device,
        mesh=mesh,
        in_specs=(
            P(("dp", "expert"), "tensor"),
            P(("dp", "expert"), None),
            P(("dp", "expert"), None),
            P(("dp", "expert"), "tensor", None),
            P(("dp", "expert"), "tensor", None, None, None),
            P(("dp", "expert"), "tensor", None, None, None),
            P(("dp", "expert"), "tensor", None, None, None),
        ),
        out_specs=P(("dp", "expert"), "tensor"),
        check_vma=False,
    )
```

profile of v0, /device:TPU:1, one launch (start us, length us, event | category | flops | bytes accessed | tf_op | source)
XLA Modules:
  0.0 545.4 jit_solution(15346772995551788982)
XLA Ops:
  6.5 0.8 copy.77
  7.3 0.1 eq.91
  7.4 0.1 eq.87
  7.5 0.1 copy.79
  7.6 0.2 fusion.125
  8.0 0.2 fusion.116
  8.2 0.1 reshape.62
  8.4 0.7 multiply_add_fusion
  9.1 0.5 fusion.21
  9.7 1.8 convolution_convert_fusion
  11.5 2.5 reshape.63
  14.0 73.0 %all_to_all.19 = bf16[128,6,1024]{2,1,0:T(8,128)(2,1)} all-to-all(bf16[128,6,1024]{2,1,0:T(8,128)(2,1)S(1)} %reshape.63), channel_id=1, replica_groups=mesh['dp'=16,'expert'=8,'tensor'=4] {'dp','expert'}, dimensions={0} | all-to-all | bytes 3145728 | tf_op jit(solution)/shard_map/all_to_all | solution.py:37
  87.0 81.0 %all-gather.2.cloned.1.call-done = bf16[128,6,4096]{2,1,0:T(8,128)(2,1)} async-done(((bf16[128,6,1024]{2,1,0:T(8,128)(2,1)}), bf16[128,6,4096]{2,1,0:T(8,128)(2,1)}) %all-gather.2.cloned.1.call-update) | async-done | bytes 6291472 | tf_op jit(solution)/shard_map/all_gather | solution.py:38
  168.1 13.8 %reshape.64 = bf16[768,32,128]{2,1,0:T(8,128)(2,1)} reshape(bf16[128,6,4096]{2,1,0:T(8,128)(2,1)} %all-gather.2.cloned.1.call-done) | data formatting | bytes 12582912 | tf_op jit(solution)/shard_map/reshape | solution.py:42
  181.9 7.9 %copy.83 = bf16[768,32,128]{2,0,1:T(8,128)(2,1)} copy(bf16[768,32,128]{2,1,0:T(8,128)(2,1)} %reshape.64) | data formatting | bytes 12582912 | tf_op jit(solution)/shard_map/reshape | solution.py:42
  189.7 5.2 gather_fusion.1
  194.9 3.8 gather_fusion.2
  198.7 2.5 fusion.28
  201.2 1.8 fusion.34
  203.0 6.5 %fusion.71 = f32[768,12,128]{2,0,1:T(8,128)} fusion(bf16[12,768,128]{2,1,0:T(8,128)(2,1)} %gather_fusion.1, pred[12]{0:T(512)(128)(4,1)S(1)} %get-tuple-element.56, bf16[1,3,12,128,128]{4,3,2,1,0:T(8,128)(2,1)} %param.17, bf16[1,3,12,128,128]{4,3,2,1,0:T(8,128)(2,1)} %param.16, f32[768,128]{1,0:T(8,128)S(1)} %fusion.28), kind=kOutput, calls=%fused_computation.54 | convolution fusion | flops 605749248 | bytes 8257548 | tf_op jit(solution)/shard_map/rf,kfc->rkc/dot_general | solution.py:55
  209.5 5.8 %fusion.74 = f32[768,12,128]{2,0,1:T(8,128)} fusion(bf16[12,768,128]{2,1,0:T(8,128)(2,1)S(1)} %gather_fusion.2, pred[12]{0:T(512)(128)(4,1)S(1)} %get-tuple-element.54, bf16[1,3,12,128,128]{4,3,2,1,0:T(8,128)(2,1)} %param.17, bf16[1,3,12,128,128]{4,3,2,1,0:T(8,128)(2,1)} %param.16, f32[768,128]{1,0:T(8,128)S(1)} %fusion.34), kind=kOutput, calls=%fused_computation.55 | convolution fusion | flops 605749248 | bytes 8257548 | tf_op jit(solution)/shard_map/rf,kfc->rkc/dot_general | solution.py:55
  215.3 3.8 gather_fusion
  219.1 1.4 copy-done.2
  220.5 1.8 fusion.22
  222.3 6.6 %fusion.68 = f32[768,12,128]{2,0,1:T(8,128)} fusion(bf16[12,768,128]{2,1,0:T(8,128)(2,1)} %copy-done.2, pred[12]{0:T(512)(128)(4,1)S(1)} %get-tuple-element.23, bf16[1,3,12,128,128]{4,3,2,1,0:T(8,128)(2,1)} %param.17, bf16[1,3,12,128,128]{4,3,2,1,0:T(8,128)(2,1)} %param.16, f32[768,128]{1,0:T(8,128)S(1)} %fusion.22), kind=kOutput, calls=%fused_computation.53 | convolution fusion | flops 605749248 | bytes 8257548 | tf_op jit(solution)/shard_map/rf,kfc->rkc/dot_general | solution.py:55
  229.0 13.8 %fusion.3 = f32[32,768,128]{2,0,1:T(8,128)} fusion(f32[768,12,128]{2,0,1:T(8,128)} %fusion.71, s32[12]{0:T(128)S(1)} %get-tuple-element.53), kind=kOutput, calls=%fused_computation.16 | convolution fusion | flops 452985216 | bytes 17301552 | tf_op jit(solution)/shard_map/rkc,kb->rbc/dot_general | solution.py:59
  242.7 12.7 %fusion.1 = f32[32,768,128]{2,0,1:T(8,128)} fusion(f32[768,12,128]{2,0,1:T(8,128)S(1)} %bitcast.217, s32[12]{0:T(128)S(1)} %get-tuple-element.52), kind=kOutput, calls=%fused_computation.14 | convolution fusion | flops 452985216 | bytes 17301552 | tf_op jit(solution)/shard_map/rkc,kb->rbc/dot_general | solution.py:59
  255.5 17.1 %fusion = bf16[768,32,128]{2,1,0:T(8,128)(2,1)} fusion(f32[32,768,128]{2,0,1:T(8,128)} %fusion.1, f32[32,768,128]{2,0,1:T(8,128)} %fusion.3, f32[768,12,128]{2,0,1:T(8,128)S(1)} %bitcast.215, s32[12]{0:T(128)S(1)} %get-tuple-element.51), kind=kOutput, calls=%fused_computation.13 | convolution fusion | flops 462422400 | bytes 36175920 | tf_op jit(solution)/shard_map/rkc,kb->rbc/dot_general | solution.py:59
  272.6 13.3 %convert_element_type.51 = bf16[128,6,4096]{2,1,0:T(8,128)(2,1)} reshape(bf16[768,32,128]{2,1,0:T(8,128)(2,1)} %fusion) | data formatting | bytes 12582912 | tf_op jit(solution)/shard_map/convert_element_type | solution.py:63
  285.9 12.8 %copy.89 = bf16[1,128,6,4096]{1,2,0,3:T(8,128)(2,1)} copy(bf16[1,128,6,4096]{3,2,1,0:T(8,128)(2,1)} %bitcast.213) | data formatting | bytes 12582912 | tf_op jit(solution)/shard_map/reshape | solution.py:66
  298.7 96.9 %all_to_all.20 = bf16[1,128,6,4096]{1,2,0,3:T(8,128)(2,1)S(1)} all-to-all(bf16[1,128,6,4096]{1,2,0,3:T(8,128)(2,1)} %copy.89), channel_id=1, replica_groups=mesh['dp'=16,'expert'=8,'tensor'=4] {'tensor'}, dimensions={3} | all-to-all | bytes 12582912 | tf_op jit(solution)/shard_map/all_to_all | solution.py:65
  395.6 3.5 copy.90
  399.1 4.1 convert_reduce_fusion
  403.1 3.5 copy.91
  406.6 16.1 %all-to-all-start.2 = ((f32[128,6,1024]{2,1,0:T(8,128)}), f32[128,6,1024]{2,1,0:T(8,128)}, u32[]{:S(2)}, u32[]{:S(2)}) async-start(f32[128,6,1024]{2,1,0:T(8,128)} %copy.91), calls=%async_computation.2 | async-start | bytes 8388608 | tf_op jit(solution)/shard_map/all_to_all | solution.py:73
  422.7 0.6 compare_and_fusion.7
  423.4 0.6 slice_bitcast_fusion.11
  424.0 98.6 %all-to-all-done.2 = f32[128,6,1024]{2,1,0:T(8,128)} async-done(((f32[128,6,1024]{2,1,0:T(8,128)}), f32[128,6,1024]{2,1,0:T(8,128)}, u32[]{:S(2)}, u32[]{:S(2)}) %all-to-all-start.2) | async-done | bytes 3145760 | tf_op jit(solution)/shard_map/all_to_all | solution.py:73
  522.6 3.1 reshape.66
  525.6 0.7 gather_fusion.3
  526.3 1.4 gather_fusion.4
  527.7 1.4 gather_fusion.5
  529.1 1.4 gather_fusion.6
  530.4 1.4 gather_fusion.7
  531.8 1.4 gather_fusion.8
  533.2 1.4 gather_fusion.9
  534.6 1.4 gather_fusion.10
  535.9 2.4 fusion.118
  (39 shorter events, 0.3 us)
Async XLA Ops:
  6.5 3.2 copy-start
  6.5 161.6 %all-gather.2.cloned.1.call-start = ((), (), s32[]{:S(2)}) async-start(), calls=%async_computation.3 | async-start | bytes 10485760 | tf_op jit(solution)/shard_map/all_gather | solution.py:38
  14.0 73.0 %copy-start.3 = (s32[1,3,12]{2,0,1:T(1,128)S(1)}, s32[1,3,12]{2,0,1:T(1,128)}, u32[]{:S(2)}) copy-start(s32[1,3,12]{2,0,1:T(1,128)} %param.14) | copy-start | bytes 436
  219.1 1.4 copy-start.2
  222.3 20.4 %slice-start.2 = ((s8[4718592]{0:T(1024)(128)(4,1)}), s8[524288]{0:T(1024)(128)(4,1)S(1)}, s32[]{:S(2)}) async-start(s8[4718592]{0:T(1024)(128)(4,1)} %bitcast.216), calls=%async_computation.6 | async-start | bytes 1048576
  228.9 13.8 %slice-start.3 = ((s8[4718592]{0:T(1024)(128)(4,1)}), s8[4194304]{0:T(1024)(128)(4,1)S(1)}, s32[]{:S(2)}) async-start(s8[4718592]{0:T(1024)(128)(4,1)} %bitcast.216), calls=%async_computation.7 | async-start | bytes 8388608
  229.0 26.5 %slice-start = ((s8[4718592]{0:T(1024)(128)(4,1)}), s8[4194304]{0:T(1024)(128)(4,1)S(1)}, s32[]{:S(2)}) async-start(s8[4718592]{0:T(1024)(128)(4,1)} %bitcast.214), calls=%async_computation.4 | async-start | bytes 8388608
  242.7 12.8 %slice-start.1 = ((s8[4718592]{0:T(1024)(128)(4,1)}), s8[524288]{0:T(1024)(128)(4,1)S(1)}, s32[]{:S(2)}) async-start(s8[4718592]{0:T(1024)(128)(4,1)} %bitcast.214), calls=%async_computation.5 | async-start | bytes 1048576
  406.6 16.8 %copy-start.4 = (f32[64,8]{0,1:T(8,128)S(1)}, f32[64,8]{0,1:T(8,128)}, u32[]{:S(2)}) copy-start(f32[64,8]{0,1:T(8,128)} %param.13) | copy-start | bytes 6148
  406.6 116.0 %all-to-all-start.2 = ((f32[128,6,1024]{2,1,0:T(8,128)}), f32[128,6,1024]{2,1,0:T(8,128)}, u32[]{:S(2)}, u32[]{:S(2)}) async-start(f32[128,6,1024]{2,1,0:T(8,128)} %copy.91), calls=%async_computation.2 | async-start | bytes 8388608 | tf_op jit(solution)/shard_map/all_to_all | solution.py:73
  533.2 5.1 copy-start.1
  534.6 1.4 copy-start.5
Sparse Core Ops, SparseCore 0:
  87.1 80.9 all-gather.1
where the time goes:
time: 550 us; the launch traced here: 545 us
  waiting for transfers between devices  180 us (33%)
  blocking collectives  170 us (31%)
  local copies, waits for them, and re-layouts  86.6 us (16%)
  matrix products  70.4 us (13%)
  starting transfers between devices  16.1 us (3%)
  between operations  13.9 us (3%)
  other arithmetic  8.84 us (2%)
    all_to_all x1, waiting for transfers between devices, per_device(): lax.all_to_all(summed, ('dp', 'expert'), split_axis=0, concat_axis=0, til...  98.6 us
    all_to_all x1, blocking collectives, per_device(): lax.all_to_all(partial_low.reshape(1, experts, capacity, D), 'tensor', sp...  96.9 us
    all_gather x1, waiting for transfers between devices, per_device(): expert_in = lax.all_gather(arrived, 'tensor', axis=2, tiled=True)  81 us
    all_to_all x1, blocking collectives, per_device(): lax.all_to_all(outgoing, ('dp', 'expert'), split_axis=0, concat_axis=0, t...  73 us
    dot_general x3, matrix products, per_device(): jnp.einsum('rkc,kb->rbc', pieces, placer, precision=lax.Precision.HIGHEST)  43.6 us
    reshape x2, local copies, waits for them, and re-layouts, per_device(): blocked = expert_in.reshape(row_count, D // BLK, BLK)  21.6 us
    dot_general x3, matrix products, per_device(): jnp.einsum('rf,kfc->rkc', hidden, down_blocks[0, block], preferred_elemen...  18.9 us
    all_to_all x1, starting transfers between devices, per_device(): lax.all_to_all(summed, ('dp', 'expert'), split_axis=0, concat_axis=0, til...  16.1 us
  transfers between devices with their start and end apart: 2, of which 2 were waited for; matrix products, arithmetic and copies ran while one was open for 0% of the time, Pallas kernels for 0%

commit v1 on v0

--- a/solution.py
+++ b/solution.py
@@ -62,12 +62,10 @@
     partial_low = lax.optimization_barrier(
         partial_value.reshape(experts, capacity, D).astype(jnp.bfloat16)
     )
-    shares = lax.all_to_all(
-        partial_low.reshape(1, experts, capacity, D),
-        "tensor",
-        split_axis=3,
-        concat_axis=0,
-        tiled=True,
+    xin = partial_low.reshape(1, experts, capacity, D)
+    shares = jnp.concatenate(
+        lax.all_to_all(jnp.stack(jnp.split(xin, lax.axis_size("tensor"), axis=3)), "tensor", 0, 0),
+        axis=0,
     )
     summed = jnp.sum(shares.astype(jnp.float32), axis=0)
     returned_rows = lax.all_to_all(

time: 550 us -> 522 us (0.949)
  blocking collectives: 170 us -> 147 us
  local copies, waits for them, and re-layouts: 86.6 us -> 80.9 us
    all_to_all x1, blocking collectives: 96.9 us -> 74.5 us  [per_device(): lax.all_to_all(jnp.stack(jnp.split(xin, lax.axis_size('tensor'), axis=3))...]
    reshape x1 -> x0, local copies, waits for them, and re-layouts: 12.8 us -> none  [per_device(): partial_low.reshape(1, experts, capacity, D)]
    another operation x3 -> x5, local copies, waits for them, and re-layouts: 0.03 us -> 10.1 us  [the longest x2 10.1 us: per_device(): jnp.stack(jnp.split(xin, lax.axis_size('tensor'), axis=3))]
where the time goes in v1:
time: 522 us; the launch traced here: 517 us
  waiting for transfers between devices  180 us (34%)
  blocking collectives  147 us (28%)
  local copies, waits for them, and re-layouts  80.9 us (15%)
  matrix products  70.9 us (14%)
  starting transfers between devices  16.1 us (3%)
  between operations  13.9 us (3%)
  other arithmetic  8.53 us (2%)
    all_to_all x1, waiting for transfers between devices, per_device(): lax.all_to_all(summed, ('dp', 'expert'), split_axis=0, concat_axis=0, til...  98.6 us
    all_gather x1, waiting for transfers between devices, per_device(): expert_in = lax.all_gather(arrived, 'tensor', axis=2, tiled=True)  81 us
    all_to_all x1, blocking collectives, per_device(): lax.all_to_all(jnp.stack(jnp.split(xin, lax.axis_size('tensor'), axis=3))...  74.5 us
    all_to_all x1, blocking collectives, per_device(): lax.all_to_all(outgoing, ('dp', 'expert'), split_axis=0, concat_axis=0, t...  72.8 us
    dot_general x3, matrix products, per_device(): jnp.einsum('rkc,kb->rbc', pieces, placer, precision=lax.Precision.HIGHEST)  44.1 us
    reshape x2, local copies, waits for them, and re-layouts, per_device(): blocked = expert_in.reshape(row_count, D // BLK, BLK)  21.6 us
    dot_general x3, matrix products, per_device(): jnp.einsum('rf,kfc->rkc', hidden, down_blocks[0, block], preferred_elemen...  18.9 us
    all_to_all x1, starting transfers between devices, per_device(): lax.all_to_all(summed, ('dp', 'expert'), split_axis=0, concat_axis=0, til...  16.1 us
  transfers between devices with their start and end apart: 2, of which 2 were waited for; matrix products, arithmetic and copies ran while one was open for 0% of the time, Pallas kernels for 0%

profile of v1, /device:TPU:1, one launch (start us, length us, event | category | flops | bytes accessed | tf_op | source)
XLA Modules:
  0.0 517.3 jit_solution(11604110290503287347)
XLA Ops:
  6.5 0.8 copy.85
  7.3 0.1 eq.91
  7.5 0.1 copy.87
  7.6 0.2 fusion.125
  8.0 0.2 fusion.116
  8.2 0.1 reshape.60
  8.4 0.7 multiply_add_fusion
  9.1 0.5 fusion.21
  9.7 1.8 convolution_convert_fusion
  11.5 2.5 reshape.61
  14.0 72.8 %all_to_all.15 = bf16[128,6,1024]{2,1,0:T(8,128)(2,1)} all-to-all(bf16[128,6,1024]{2,1,0:T(8,128)(2,1)S(1)} %reshape.61), channel_id=1, replica_groups=mesh['dp'=16,'expert'=8,'tensor'=4] {'dp','expert'}, dimensions={0} | all-to-all | bytes 3145728 | tf_op jit(solution)/shard_map/all_to_all | solution.py:37
  86.9 81.0 %all-gather.2.cloned.1.call-done = bf16[128,6,4096]{2,1,0:T(8,128)(2,1)} async-done(((bf16[128,6,1024]{2,1,0:T(8,128)(2,1)}), bf16[128,6,4096]{2,1,0:T(8,128)(2,1)}) %all-gather.2.cloned.1.call-update) | async-done | bytes 6291472 | tf_op jit(solution)/shard_map/all_gather | solution.py:38
  167.9 13.8 %reshape.62 = bf16[768,32,128]{2,1,0:T(8,128)(2,1)} reshape(bf16[128,6,4096]{2,1,0:T(8,128)(2,1)} %all-gather.2.cloned.1.call-done) | data formatting | bytes 12582912 | tf_op jit(solution)/shard_map/reshape | solution.py:42
  181.7 7.9 %copy.91 = bf16[768,32,128]{2,0,1:T(8,128)(2,1)} copy(bf16[768,32,128]{2,1,0:T(8,128)(2,1)} %reshape.62) | data formatting | bytes 12582912 | tf_op jit(solution)/shard_map/reshape | solution.py:42
  189.6 5.2 %gather_fusion.1 = bf16[12,768,128]{2,1,0:T(8,128)(2,1)} fusion(bf16[768,32,128]{2,0,1:T(8,128)(2,1)} %copy.91, s32[1024]{0:T(1024)S(1)} %get-tuple-element.63), kind=kCustom, calls=%fused_computation.2.clone | custom fusion | bytes 4718640 | tf_op jit(solution)/shard_map/jit(_take)/gather | solution.py:47
  194.7 3.8 gather_fusion.2
  198.5 2.5 fusion.28
  201.1 1.8 fusion.34
  202.9 6.5 %fusion.71 = f32[768,12,128]{2,0,1:T(8,128)} fusion(bf16[12,768,128]{2,1,0:T(8,128)(2,1)} %gather_fusion.1, pred[12]{0:T(512)(128)(4,1)S(1)} %get-tuple-element.60, bf16[1,3,12,128,128]{4,3,2,1,0:T(8,128)(2,1)} %param.17, bf16[1,3,12,128,128]{4,3,2,1,0:T(8,128)(2,1)} %param.16, f32[768,128]{1,0:T(8,128)S(1)} %fusion.28), kind=kOutput, calls=%fused_computation.59 | convolution fusion | flops 605749248 | bytes 8257548 | tf_op jit(solution)/shard_map/rf,kfc->rkc/dot_general | solution.py:55
  209.3 5.8 %fusion.74 = f32[768,12,128]{2,0,1:T(8,128)} fusion(bf16[12,768,128]{2,1,0:T(8,128)(2,1)S(1)} %gather_fusion.2, pred[12]{0:T(512)(128)(4,1)S(1)} %get-tuple-element.58, bf16[1,3,12,128,128]{4,3,2,1,0:T(8,128)(2,1)} %param.17, bf16[1,3,12,128,128]{4,3,2,1,0:T(8,128)(2,1)} %param.16, f32[768,128]{1,0:T(8,128)S(1)} %fusion.34), kind=kOutput, calls=%fused_computation.60 | convolution fusion | flops 605749248 | bytes 8257548 | tf_op jit(solution)/shard_map/rf,kfc->rkc/dot_general | solution.py:55
  215.1 3.8 gather_fusion
  218.9 1.4 copy-done.2
  220.4 1.8 fusion.22
  222.2 6.6 %fusion.68 = f32[768,12,128]{2,0,1:T(8,128)} fusion(bf16[12,768,128]{2,1,0:T(8,128)(2,1)} %copy-done.2, pred[12]{0:T(512)(128)(4,1)S(1)} %get-tuple-element.23, bf16[1,3,12,128,128]{4,3,2,1,0:T(8,128)(2,1)} %param.17, bf16[1,3,12,128,128]{4,3,2,1,0:T(8,128)(2,1)} %param.16, f32[768,128]{1,0:T(8,128)S(1)} %fusion.22), kind=kOutput, calls=%fused_computation.58 | convolution fusion | flops 605749248 | bytes 8257548 | tf_op jit(solution)/shard_map/rf,kfc->rkc/dot_general | solution.py:55
  228.8 14.2 %fusion.3 = f32[32,768,128]{2,0,1:T(8,128)} fusion(f32[768,12,128]{2,0,1:T(8,128)} %fusion.71, s32[12]{0:T(128)S(1)} %get-tuple-element.57), kind=kOutput, calls=%fused_computation.17 | convolution fusion | flops 452985216 | bytes 17301552 | tf_op jit(solution)/shard_map/rkc,kb->rbc/dot_general | solution.py:59
  243.1 12.7 %fusion.1 = f32[32,768,128]{2,0,1:T(8,128)} fusion(f32[768,12,128]{2,0,1:T(8,128)S(1)} %bitcast.223, s32[12]{0:T(128)S(1)} %get-tuple-element.56), kind=kOutput, calls=%fused_computation.15 | convolution fusion | flops 452985216 | bytes 17301552 | tf_op jit(solution)/shard_map/rkc,kb->rbc/dot_general | solution.py:59
  255.8 17.1 %fusion = bf16[768,32,128]{2,1,0:T(8,128)(2,1)} fusion(f32[32,768,128]{2,0,1:T(8,128)} %fusion.1, f32[32,768,128]{2,0,1:T(8,128)} %fusion.3, f32[768,12,128]{2,0,1:T(8,128)S(1)} %bitcast.221, s32[12]{0:T(128)S(1)} %get-tuple-element.55), kind=kOutput, calls=%fused_computation.14 | convolution fusion | flops 462422400 | bytes 36175920 | tf_op jit(solution)/shard_map/rkc,kb->rbc/dot_general | solution.py:59
  272.9 13.3 %convert_element_type.47 = bf16[128,6,4096]{2,1,0:T(8,128)(2,1)} reshape(bf16[768,32,128]{2,1,0:T(8,128)(2,1)} %fusion) | data formatting | bytes 12582912 | tf_op jit(solution)/shard_map/convert_element_type | solution.py:63
  286.2 3.9 slice_bitcast_fusion.3
  290.1 2.3 pad_maximum_fusion
  292.3 6.2 %copy.97 = bf16[4,1,128,6,1024]{4,2,3,1,0:T(8,128)(2,1)} copy(bf16[4,1,128,6,1024]{4,3,2,1,0:T(8,128)(2,1)S(1)} %pad_maximum_fusion) | data formatting | bytes 12582912 | tf_op jit(solution)/shard_map/stack | solution.py:67
  298.5 74.5 %all_to_all.16 = bf16[4,1,128,6,1024]{4,2,3,1,0:T(8,128)(2,1)S(1)} all-to-all(bf16[4,1,128,6,1024]{4,2,3,1,0:T(8,128)(2,1)} %copy.97), channel_id=1, replica_groups=mesh['dp'=16,'expert'=8,'tensor'=4] {'tensor'}, dimensions={0} | all-to-all | bytes 12582912 | tf_op jit(solution)/shard_map/all_to_all | solution.py:67
  373.0 1.5 convert_reduce_fusion
  374.5 3.9 copy.98
  378.4 16.1 %all-to-all-start.2 = ((f32[128,6,1024]{2,1,0:T(8,128)}), f32[128,6,1024]{2,1,0:T(8,128)}, u32[]{:S(2)}, u32[]{:S(2)}) async-start(f32[128,6,1024]{2,1,0:T(8,128)} %copy.98), calls=%async_computation.2 | async-start | bytes 8388608 | tf_op jit(solution)/shard_map/all_to_all | solution.py:71
  394.5 0.6 compare_and_fusion.7
  395.1 0.6 slice_bitcast_fusion.15
  395.7 98.6 %all-to-all-done.2 = f32[128,6,1024]{2,1,0:T(8,128)} async-done(((f32[128,6,1024]{2,1,0:T(8,128)}), f32[128,6,1024]{2,1,0:T(8,128)}, u32[]{:S(2)}, u32[]{:S(2)}) %all-to-all-start.2) | async-done | bytes 3145760 | tf_op jit(solution)/shard_map/all_to_all | solution.py:71
  494.4 3.1 reshape.64
  497.4 0.7 gather_fusion.3
  498.1 1.4 gather_fusion.4
  499.5 1.4 gather_fusion.5
  500.9 1.4 gather_fusion.6
  502.2 1.4 gather_fusion.7
  503.6 1.4 gather_fusion.8
  505.0 1.4 gather_fusion.9
  506.4 1.4 gather_fusion.10
  507.8 2.4 fusion.118
  (40 shorter events, 0.4 us)
Async XLA Ops:
  6.5 3.2 copy-start
  6.5 161.4 %all-gather.2.cloned.1.call-start = ((), (), s32[]{:S(2)}) async-start(), calls=%async_computation.3 | async-start | bytes 10485760 | tf_op jit(solution)/shard_map/all_gather | solution.py:38
  14.0 72.8 %copy-start.3 = (s32[1,3,12]{2,0,1:T(1,128)S(1)}, s32[1,3,12]{2,0,1:T(1,128)}, u32[]{:S(2)}) copy-start(s32[1,3,12]{2,0,1:T(1,128)} %param.14) | copy-start | bytes 436
  218.9 1.4 copy-start.2
  222.2 20.9 %slice-start.2 = ((s8[4718592]{0:T(1024)(128)(4,1)}), s8[524288]{0:T(1024)(128)(4,1)S(1)}, s32[]{:S(2)}) async-start(s8[4718592]{0:T(1024)(128)(4,1)} %bitcast.222), calls=%async_computation.6 | async-start | bytes 1048576
  228.8 14.3 %slice-start.3 = ((s8[4718592]{0:T(1024)(128)(4,1)}), s8[4194304]{0:T(1024)(128)(4,1)S(1)}, s32[]{:S(2)}) async-start(s8[4718592]{0:T(1024)(128)(4,1)} %bitcast.222), calls=%async_computation.7 | async-start | bytes 8388608
  228.8 27.0 %slice-start = ((s8[4718592]{0:T(1024)(128)(4,1)}), s8[4194304]{0:T(1024)(128)(4,1)S(1)}, s32[]{:S(2)}) async-start(s8[4718592]{0:T(1024)(128)(4,1)} %bitcast.220), calls=%async_computation.4 | async-start | bytes 8388608
  243.1 12.8 %slice-start.1 = ((s8[4718592]{0:T(1024)(128)(4,1)}), s8[524288]{0:T(1024)(128)(4,1)S(1)}, s32[]{:S(2)}) async-start(s8[4718592]{0:T(1024)(128)(4,1)} %bitcast.220), calls=%async_computation.5 | async-start | bytes 1048576
  378.4 16.7 %copy-start.4 = (f32[64,8]{0,1:T(8,128)S(1)}, f32[64,8]{0,1:T(8,128)}, u32[]{:S(2)}) copy-start(f32[64,8]{0,1:T(8,128)} %param.13) | copy-start | bytes 6148
  378.4 116.0 %all-to-all-start.2 = ((f32[128,6,1024]{2,1,0:T(8,128)}), f32[128,6,1024]{2,1,0:T(8,128)}, u32[]{:S(2)}, u32[]{:S(2)}) async-start(f32[128,6,1024]{2,1,0:T(8,128)} %copy.98), calls=%async_computation.2 | async-start | bytes 8388608 | tf_op jit(solution)/shard_map/all_to_all | solution.py:71
  505.0 5.2 copy-start.1
  506.4 1.4 copy-start.5
Sparse Core Ops, SparseCore 0:
  86.9 80.9 all-gather.1
